TPU v7x, 256 devices: a whole 4x4x8 slice. The times are simulated.
256 devices in a mesh: row: 16 (over z, core), col: 16 (over y, x).
Axes of the slice: x: 4, y: 4, z: 8, core: 2. Of those that a mesh axis runs over, the one named last changes fastest.
Arguments:
- start_basis: float32 [32, 131072], P(None, ('row', 'col')), may hold values from -6 to 6
- degrees: float32 [131072], P(('row', 'col')), may hold values from 0.5 to 1.5
- tiles: float32 [8192, 256, 256], P(('row', 'col')), may hold values from -0.046875 to 0.046875
- tile_rows: int32 [16, 512], P('row', 'col'), may hold values from 0 to 31, as said below
- tile_cols: int32 [16, 512], P('row', 'col'), may hold values from 0 to 31
- counts: int32 [16, 16], P('row', 'col'), may hold values from 1 to 31, as said below
Outputs:
- basis: float32 [32, 131072], P(None, ('row', 'col'))
- projected: float32 [32, 32], replicated
Inputs may be any that keep to these rules, and one draw needn't show every extreme that they name: `tile_rows`: the 32 (row, column) pairs of one device are distinct. counts[r, c] + counts[r', c] <= 32 where r' differs from r by 8; equality holds in column 0.
All inputs are finite; a program needn't handle non-finite values.
Results may differ from a plain program's by a relative error of at most 0.0003.
Values sent between devices are 32-bit elements; how exact they have to be, the bound alone decides.
A program may use at most 64 MiB of HBM per device.

v0:
```python
import jax
import jax.numpy as jnp
from jax import lax
from jax.sharding import PartitionSpec as P

DEGREE = 3
center_shift = 1.0
spread_radius = 1.4
group_width = 8


def tile_products(blocks, tiles, row_local, col_local, live, row_blocks):
    subspace = blocks.shape[0]
    edge = blocks.shape[2]
    block_ids = jnp.arange(row_blocks, dtype=jnp.int32)

    def add_group(index, total):
        start = index * group_width
        group_tiles = lax.dynamic_slice_in_dim(tiles, start, group_width, 0)
        group_rows = lax.dynamic_slice_in_dim(row_local, start, group_width, 0)
        group_cols = lax.dynamic_slice_in_dim(col_local, start, group_width, 0)
        picked = jnp.take(blocks, group_cols, axis=1)
        product = jnp.einsum("kgj,gij->kgi", picked, group_tiles, precision=lax.Precision.HIGHEST)
        valid = start + jnp.arange(group_width, dtype=jnp.int32) < live
        select = ((group_rows[None, :] == block_ids[:, None]) & valid[None, :]).astype(jnp.float32)
        return total + jnp.einsum("ig,kgb->kib", select, product, precision=lax.Precision.HIGHEST)

    initial = jnp.zeros((subspace, row_blocks, edge), jnp.float32)
    return lax.fori_loop(0, (live + group_width - 1) // group_width, add_group, initial)


def inner_products(left, right):
    return jnp.einsum("kn,mn->km", left, right, precision=lax.Precision.HIGHEST)


def body(start_basis, degrees, tiles, tile_rows, tile_cols, counts):
    subspace = start_basis.shape[0]
    edge = tiles.shape[1]
    row_local = tile_rows[0]
    col_local = tile_cols[0]
    live_count = counts[0, 0]
    row_blocks = lax.axis_size("col") * start_basis.shape[1] // edge
    nverts = lax.axis_size("row") * lax.axis_size("col") * start_basis.shape[1]

    def apply_operator(vectors):
        gathered = lax.all_gather(vectors, "row", axis=1, tiled=True)
        blocks = gathered.reshape(subspace, -1, edge)
        partial_value = tile_products(blocks, tiles, row_local, col_local, live_count, row_blocks)
        summed = lax.psum_scatter(
            partial_value.reshape(subspace, -1), "col", scatter_dimension=1, tiled=True
        )
        return degrees[None, :] * vectors - summed

    def shifted(vectors):
        return (apply_operator(vectors) - center_shift * vectors) / spread_radius

    previous = start_basis
    filtered = shifted(start_basis)
    for level in range(DEGREE - 1):
        following = 2.0 * shifted(filtered) - previous
        previous, filtered = (filtered, following)
    gram_matrix = lax.psum(inner_products(filtered, filtered), ("row", "col")) / nverts
    factor = jnp.linalg.cholesky(gram_matrix)
    basis = jax.scipy.linalg.solve_triangular(factor, filtered, lower=True)
    image = apply_operator(basis)
    moment = lax.psum(inner_products(basis, image), ("row", "col")) / nverts
    projected = 0.5 * (moment + moment.T)
    return (basis, projected)


def solution(mesh):
    return jax.shard_map(
        body,
        mesh=mesh,
        in_specs=(
            P(None, ("row", "col")),
            P(("row", "col")),
            P(("row", "col"), None, None),
            P("row", "col"),
            P("row", "col"),
            P("row", "col"),
        ),
        out_specs=(P(None, ("row", "col")), P()),
        check_vma=False,
    )
```

profile of v0, /device:TPU:1, one launch (start us, length us, event | category | flops | bytes accessed | tf_op | source)
XLA Modules:
  0.0 776.5 jit_solution(2379847340742066916)
XLA Ops:
  8.6 44.0 %all-gather.5.cloned.1.call-done = f32[32,8192]{1,0:T(8,128)} async-done(((f32[32,512]{1,0:T(8,128)}), f32[32,8192]{1,0:T(8,128)}) %all-gather.5.cloned.1.call-update) | async-done | bytes 1048592 | tf_op jit(solution)/shard_map/all_gather | solution.py:46
  54.1 29.0 %while.44 = (s32[]{:T(128)}, f32[32,32,256]{2,1,0:T(8,128)S(1)}, s32[]{:T(128)}, f32[32,256,256]{2,1,0:T(8,128)}, s32[32]{0:T(128)}, /*index=5*/f32[32,32,256]{2...) while((s32[]{:T(128)}, f32[32,32,256]{2,1,0:T(8,128)S(1)}, ...), condition=%wide.region_1.3_spmd.clone, body=%wide.region_0.2_spmd.clone.sunk | while | flops 226821696 | bytes 5509559 | solution.py:29
  56.1 3.6 fusion.122
  63.4 3.6 fusion.122
  70.6 3.6 fusion.122
  77.9 3.6 fusion.122
  84.8 75.6 %reduce-scatter.5.cloned.1.call-done = f32[32,512]{1,0:T(8,128)} async-done(((f32[32,8192]{1,0:T(8,128)}), f32[32,512]{1,0:T(8,128)}) %reduce-scatter.5.cloned.1.call-update) | async-done | bytes 65552 | tf_op jit(solution)/shard_map/reduce_scatter | solution.py:49
  161.9 41.0 %all-gather.7.cloned.1.call-done = f32[32,8192]{1,0:T(8,128)} async-done(((f32[32,512]{1,0:T(8,128)}), f32[32,8192]{1,0:T(8,128)}) %all-gather.7.cloned.1.call-update) | async-done | bytes 1048592 | tf_op jit(solution)/shard_map/all_gather | solution.py:46
  204.4 29.0 %while.45 = (s32[]{:T(128)}, f32[32,32,256]{2,1,0:T(8,128)S(1)}, s32[]{:T(128)}, f32[32,256,256]{2,1,0:T(8,128)}, s32[32]{0:T(128)}, /*index=5*/f32[32,32,256]{2...) while((s32[]{:T(128)}, f32[32,32,256]{2,1,0:T(8,128)S(1)}, ...), condition=%wide.region_4.6_spmd.clone, body=%wide.region_3.5_spmd.clone.sunk | while | flops 226821696 | bytes 5509559 | solution.py:29
  206.4 3.6 fusion.128
  213.6 3.6 fusion.128
  220.9 3.6 fusion.128
  228.1 3.6 fusion.128
  235.1 75.6 %reduce-scatter.7.cloned.1.call-done = f32[32,512]{1,0:T(8,128)} async-done(((f32[32,8192]{1,0:T(8,128)}), f32[32,512]{1,0:T(8,128)}) %reduce-scatter.7.cloned.1.call-update) | async-done | bytes 65552 | tf_op jit(solution)/shard_map/reduce_scatter | solution.py:49
  312.3 40.8 %all-gather.9.cloned.1.call-done = f32[32,8192]{1,0:T(8,128)} async-done(((f32[32,512]{1,0:T(8,128)}), f32[32,8192]{1,0:T(8,128)}) %all-gather.9.cloned.1.call-update) | async-done | bytes 1048592 | tf_op jit(solution)/shard_map/all_gather | solution.py:46
  354.6 29.0 %while.46 = (s32[]{:T(128)}, f32[32,32,256]{2,1,0:T(8,128)S(1)}, s32[]{:T(128)}, f32[32,256,256]{2,1,0:T(8,128)}, s32[32]{0:T(128)}, /*index=5*/f32[32,32,256]{2...) while((s32[]{:T(128)}, f32[32,32,256]{2,1,0:T(8,128)S(1)}, ...), condition=%wide.region_7.9_spmd.clone, body=%wide.region_6.8_spmd.clone.sunk | while | flops 226821696 | bytes 5509559 | solution.py:29
  356.6 3.6 fusion.134
  363.8 3.6 fusion.134
  371.1 3.6 fusion.134
  378.3 3.6 fusion.134
  385.3 75.6 %reduce-scatter.9.cloned.1.call-done = f32[32,512]{1,0:T(8,128)} async-done(((f32[32,8192]{1,0:T(8,128)}), f32[32,512]{1,0:T(8,128)}) %reduce-scatter.9.cloned.1.call-update) | async-done | bytes 65552 | tf_op jit(solution)/shard_map/reduce_scatter | solution.py:49
  462.0 77.5 %psum.14 = f32[32,32]{0,1:T(8,128)S(1)} all-reduce(f32[32,32]{0,1:T(8,128)S(1)} %fusion.89), channel_id=1, replica_groups=mesh['row'=16,'col'=16] {'row','col'}, use_global_device_ids=true, to_apply=%region_9.11 | all-reduce | flops 1024 | bytes 8192 | tf_op jit(solution)/shard_map/psum | solution.py:62
  539.6 2.9 cholesky.16
  543.9 2.4 custom-call.7
  547.3 35.6 %all-gather.11.cloned.1.call-done = f32[32,8192]{1,0:T(8,128)} async-done(((f32[32,512]{1,0:T(8,128)}), f32[32,8192]{1,0:T(8,128)}) %all-gather.11.cloned.1.call-update) | async-done | bytes 1048592 | tf_op jit(solution)/shard_map/all_gather | solution.py:46
  584.4 29.0 %while.47 = (s32[]{:T(128)}, f32[32,32,256]{2,1,0:T(8,128)S(1)}, s32[]{:T(128)}, f32[32,256,256]{2,1,0:T(8,128)}, s32[32]{0:T(128)}, /*index=5*/f32[32,32,256]{2...) while((s32[]{:T(128)}, f32[32,32,256]{2,1,0:T(8,128)S(1)}, ...), condition=%wide.region_13.15_spmd.clone, body=%wide.region_12.14_spmd.clone.sunk | while | flops 226821696 | bytes 5509559 | solution.py:29
  586.4 3.6 fusion.140
  593.6 3.6 fusion.140
  600.9 3.6 fusion.140
  608.1 3.6 fusion.140
  615.0 75.7 %reduce-scatter.11.cloned.1.call-done = f32[32,512]{1,0:T(8,128)} async-done(((f32[32,8192]{1,0:T(8,128)}), f32[32,512]{1,0:T(8,128)}) %reduce-scatter.11.cloned.1.call-update) | async-done | bytes 65552 | tf_op jit(solution)/shard_map/reduce_scatter | solution.py:49
  691.7 77.3 %psum.15 = f32[32,32]{0,1:T(8,128)S(1)} all-reduce(f32[32,32]{0,1:T(8,128)S(1)} %fusion.80), channel_id=1, replica_groups=mesh['row'=16,'col'=16] {'row','col'}, use_global_device_ids=true, to_apply=%region_15.17 | all-reduce | flops 1024 | bytes 8192 | tf_op jit(solution)/shard_map/psum | solution.py:66
  (136 shorter events, 78.6 us)
Async XLA Ops:
  7.2 45.4 %all-gather.5.cloned.1.call-start = ((), (), s32[]{:S(2)}) async-start(), calls=%async_computation.4 | async-start | bytes 1114112 | tf_op jit(solution)/shard_map/all_gather | solution.py:46
  7.9 152.5 %reduce-scatter.5.cloned.1.call-start = ((), (), s32[]{:S(2)}) async-start(), calls=%async_computation.5 | async-start | bytes 1114112 | tf_op jit(solution)/shard_map/reduce_scatter | solution.py:49
  54.1 106.3 %copy-start = (f32[32,512]{1,0:T(8,128)S(1)}, f32[32,512]{1,0:T(8,128)}, u32[]{:S(2)}) copy-start(f32[32,512]{1,0:T(8,128)} %param.16) | copy-start | bytes 196612
  54.1 106.3 %copy-start.4 = (f32[512]{0:T(512)S(1)}, f32[512]{0:T(512)}, u32[]{:S(2)}) copy-start(f32[512]{0:T(512)} %param.17) | copy-start | bytes 6148
  84.7 118.2 %all-gather.7.cloned.1.call-start = ((), (), s32[]{:S(2)}) async-start(), calls=%async_computation.6 | async-start | bytes 1114112 | tf_op jit(solution)/shard_map/all_gather | solution.py:46
  161.9 148.8 %reduce-scatter.7.cloned.1.call-start = ((), (), s32[]{:S(2)}) async-start(), calls=%async_computation.7 | async-start | bytes 1114112 | tf_op jit(solution)/shard_map/reduce_scatter | solution.py:49
  204.4 106.3 %copy-start.2 = (f32[32,512]{1,0:T(8,128)S(1)}, f32[32,512]{1,0:T(8,128)}, u32[]{:S(2)}) copy-start(f32[32,512]{1,0:T(8,128)} %reduce-scatter.5.cloned.1.call-done) | copy-start | bytes 196612
  235.0 118.1 %all-gather.9.cloned.1.call-start = ((), (), s32[]{:S(2)}) async-start(), calls=%async_computation.8 | async-start | bytes 1114112 | tf_op jit(solution)/shard_map/all_gather | solution.py:46
  312.2 148.7 %reduce-scatter.9.cloned.1.call-start = ((), (), s32[]{:S(2)}) async-start(), calls=%async_computation.9 | async-start | bytes 1114112 | tf_op jit(solution)/shard_map/reduce_scatter | solution.py:49
  354.6 106.3 %copy-start.3 = (f32[32,512]{1,0:T(8,128)S(1)}, f32[32,512]{1,0:T(8,128)}, u32[]{:S(2)}) copy-start(f32[32,512]{1,0:T(8,128)} %multiply_subtract_fusion.1) | copy-start | bytes 196612
  385.2 197.7 %all-gather.11.cloned.1.call-start = ((), (), s32[]{:S(2)}) async-start(), calls=%async_computation.10 | async-start | bytes 1114112 | tf_op jit(solution)/shard_map/all_gather | solution.py:46
  547.2 143.5 %reduce-scatter.11.cloned.1.call-start = ((), (), s32[]{:S(2)}) async-start(), calls=%async_computation.11 | async-start | bytes 1114112 | tf_op jit(solution)/shard_map/reduce_scatter | solution.py:49
  584.4 106.3 %copy-start.1 = (f32[32,512]{1,0:T(8,128)S(1)}, f32[32,512]{1,0:T(8,128)}, u32[]{:S(2)}) copy-start(f32[32,512]{1,0:T(8,128)} %fusion.87) | copy-start | bytes 196612
Sparse Core Ops, SparseCore 0:
  9.8 42.7 all-gather.4
  84.9 75.4 reduce-scatter.4
  162.8 40.0 all-gather.6
  235.1 75.5 reduce-scatter.6
  313.0 40.0 all-gather.8
  385.3 75.5 reduce-scatter.8
  547.4 35.5 all-gather.10
  615.1 75.4 reduce-scatter.10
where the time goes:
time: 778 us; the launch traced here: 777 us
  waiting for transfers between devices  465 us (60%)
  blocking collectives  155 us (20%)
  matrix products  74.3 us (10%)
  other arithmetic  33.4 us (4%)
  local copies, waits for them, and re-layouts  33.2 us (4%)
  between operations  15 us (2%)
    reduce_scatter x4, waiting for transfers between devices, apply_operator(): lax.psum_scatter(partial_value.reshape(subspace, -1), 'col', scatter_dime...  303 us
    all_gather x4, waiting for transfers between devices, apply_operator(): gathered = lax.all_gather(vectors, 'row', axis=1, tiled=True)  161 us
    psum x1, blocking collectives, body(): lax.psum(inner_products(filtered, filtered), ('row', 'col')) / nverts  77.5 us
    psum x1, blocking collectives, body(): moment = lax.psum(inner_products(basis, image), ('row', 'col')) / nverts  77.3 us
    dot_general x16, matrix products, add_group(): jnp.einsum('kgj,gij->kgi', picked, group_tiles, precision=lax.Precision.H...  58.1 us
    and x16, other arithmetic, add_group(): picked = jnp.take(blocks, group_cols, axis=1)  22.1 us
  transfers between devices with their start and end apart: 8, of which 8 were waited for; matrix products, arithmetic and copies ran while one was open for 0% of the time, Pallas kernels for 0%

commit v1 on v0

--- a/solution.py
+++ b/solution.py
@@ -7,6 +7,11 @@
 center_shift = 1.0
 spread_radius = 1.4
 group_width = 8
+
+
+def zone_find(arr_in):
+    response = jnp.sum(lax.all_gather(arr_in, ("row", "col")), axis=0)
+    return response
 
 
 def tile_products(blocks, tiles, row_local, col_local, live, row_blocks):
@@ -59,7 +64,7 @@
     for level in range(DEGREE - 1):
         following = 2.0 * shifted(filtered) - previous
         previous, filtered = (filtered, following)
-    gram_matrix = lax.psum(inner_products(filtered, filtered), ("row", "col")) / nverts
+    gram_matrix = zone_find(inner_products(filtered, filtered)) / nverts
     factor = jnp.linalg.cholesky(gram_matrix)
     basis = jax.scipy.linalg.solve_triangular(factor, filtered, lower=True)
     image = apply_operator(basis)

time: 778 us -> 819 us (1.053)
  waiting for transfers between devices: 465 us -> 585 us
  blocking collectives: 155 us -> 77.3 us
    all_gather x0 -> x1, waiting for transfers between devices: none -> 120 us  [zone_find(): response = jnp.sum(lax.all_gather(arr_in, ('row', 'col')), axis=0)]
    psum x1 -> x0, blocking collectives: 77.5 us -> none  [body(): lax.psum(inner_products(filtered, filtered), ('row', 'col')) / nverts]
  transfers between devices with their start and end apart: 8 -> 9, of which waited for: 8 -> 9; matrix products, arithmetic and copies ran while one was open for 0% -> 0% of each run, Pallas kernels for 0% -> 0%
where the time goes in v1:
time: 819 us; the launch traced here: 817 us
  waiting for transfers between devices  585 us (71%)
  blocking collectives  77.3 us (9%)
  matrix products  74.9 us (9%)
  other arithmetic  33.3 us (4%)
  local copies, waits for them, and re-layouts  30.5 us (4%)
  between operations  14.7 us (2%)
    reduce_scatter x4, waiting for transfers between devices, apply_operator(): lax.psum_scatter(partial_value.reshape(subspace, -1), 'col', scatter_dime...  303 us
    all_gather x4, waiting for transfers between devices, apply_operator(): gathered = lax.all_gather(vectors, 'row', axis=1, tiled=True)  162 us
    all_gather x1, waiting for transfers between devices, zone_find(): response = jnp.sum(lax.all_gather(arr_in, ('row', 'col')), axis=0)  120 us
    psum x1, blocking collectives, body(): moment = lax.psum(inner_products(basis, image), ('row', 'col')) / nverts  77.3 us
    dot_general x16, matrix products, add_group(): jnp.einsum('kgj,gij->kgi', picked, group_tiles, precision=lax.Precision.H...  58.1 us
    and x16, other arithmetic, add_group(): picked = jnp.take(blocks, group_cols, axis=1)  19.5 us
  transfers between devices with their start and end apart: 9, of which 9 were waited for; matrix products, arithmetic and copies ran while one was open for 0% of the time, Pallas kernels for 0%

profile of v1, /device:TPU:1, one launch (start us, length us, event | category | flops | bytes accessed | tf_op | source)
XLA Modules:
  0.0 817.0 jit_solution(11961103311568205321)
XLA Ops:
  8.6 44.0 %all-gather.7.cloned.1.call-done = f32[32,8192]{1,0:T(8,128)} async-done(((f32[32,512]{1,0:T(8,128)}), f32[32,8192]{1,0:T(8,128)}) %all-gather.7.cloned.1.call-update) | async-done | bytes 1048592 | tf_op jit(solution)/shard_map/all_gather | solution.py:51
  54.1 29.0 %while.44 = (s32[]{:T(128)}, f32[32,32,256]{2,1,0:T(8,128)S(1)}, s32[]{:T(128)}, f32[32,256,256]{2,1,0:T(8,128)}, s32[32]{0:T(128)}, /*index=5*/f32[32,32,256]{2...) while((s32[]{:T(128)}, f32[32,32,256]{2,1,0:T(8,128)S(1)}, ...), condition=%wide.region_1.3_spmd.clone, body=%wide.region_0.2_spmd.clone.sunk | while | flops 226821696 | bytes 5509559 | solution.py:34
  56.1 3.6 fusion.123
  63.4 3.6 fusion.123
  70.6 3.6 fusion.123
  77.9 3.6 fusion.123
  84.8 75.6 %reduce-scatter.5.cloned.1.call-done = f32[32,512]{1,0:T(8,128)} async-done(((f32[32,8192]{1,0:T(8,128)}), f32[32,512]{1,0:T(8,128)}) %reduce-scatter.5.cloned.1.call-update) | async-done | bytes 65552 | tf_op jit(solution)/shard_map/reduce_scatter | solution.py:54
  161.9 41.0 %all-gather.9.cloned.1.call-done = f32[32,8192]{1,0:T(8,128)} async-done(((f32[32,512]{1,0:T(8,128)}), f32[32,8192]{1,0:T(8,128)}) %all-gather.9.cloned.1.call-update) | async-done | bytes 1048592 | tf_op jit(solution)/shard_map/all_gather | solution.py:51
  204.4 29.0 %while.45 = (s32[]{:T(128)}, f32[32,32,256]{2,1,0:T(8,128)S(1)}, s32[]{:T(128)}, f32[32,256,256]{2,1,0:T(8,128)}, s32[32]{0:T(128)}, /*index=5*/f32[32,32,256]{2...) while((s32[]{:T(128)}, f32[32,32,256]{2,1,0:T(8,128)S(1)}, ...), condition=%wide.region_4.6_spmd.clone, body=%wide.region_3.5_spmd.clone.sunk | while | flops 226821696 | bytes 5509559 | solution.py:34
  206.4 3.6 fusion.129
  213.6 3.6 fusion.129
  220.9 3.6 fusion.129
  228.2 3.6 fusion.129
  235.1 75.6 %reduce-scatter.7.cloned.1.call-done = f32[32,512]{1,0:T(8,128)} async-done(((f32[32,8192]{1,0:T(8,128)}), f32[32,512]{1,0:T(8,128)}) %reduce-scatter.7.cloned.1.call-update) | async-done | bytes 65552 | tf_op jit(solution)/shard_map/reduce_scatter | solution.py:54
  312.3 40.8 %all-gather.11.cloned.1.call-done = f32[32,8192]{1,0:T(8,128)} async-done(((f32[32,512]{1,0:T(8,128)}), f32[32,8192]{1,0:T(8,128)}) %all-gather.11.cloned.1.call-update) | async-done | bytes 1048592 | tf_op jit(solution)/shard_map/all_gather | solution.py:51
  354.6 29.0 %while.46 = (s32[]{:T(128)}, f32[32,32,256]{2,1,0:T(8,128)S(1)}, s32[]{:T(128)}, f32[32,256,256]{2,1,0:T(8,128)}, s32[32]{0:T(128)}, /*index=5*/f32[32,32,256]{2...) while((s32[]{:T(128)}, f32[32,32,256]{2,1,0:T(8,128)S(1)}, ...), condition=%wide.region_7.9_spmd.clone, body=%wide.region_6.8_spmd.clone.sunk | while | flops 226821696 | bytes 5509559 | solution.py:34
  356.5 3.6 fusion.135
  363.8 3.6 fusion.135
  371.0 3.6 fusion.135
  378.3 3.6 fusion.135
  385.3 75.6 %reduce-scatter.9.cloned.1.call-done = f32[32,512]{1,0:T(8,128)} async-done(((f32[32,8192]{1,0:T(8,128)}), f32[32,512]{1,0:T(8,128)}) %reduce-scatter.9.cloned.1.call-update) | async-done | bytes 65552 | tf_op jit(solution)/shard_map/reduce_scatter | solution.py:54
  462.8 119.6 %all-gather.15.cloned.1.call-done = f32[8192,32]{1,0:T(8,128)} async-done(((f32[32,32]{1,0:T(8,128)}), f32[8192,32]{1,0:T(8,128)}) %all-gather.15.cloned.1.call-update) | async-done | bytes 1048592 | tf_op jit(solution)/shard_map/all_gather | solution.py:13
  582.5 2.5 reduce_sum.11
  585.1 2.9 cholesky.16
  592.8 36.1 %all-gather.13.cloned.1.call-done = f32[32,8192]{1,0:T(8,128)} async-done(((f32[32,512]{1,0:T(8,128)}), f32[32,8192]{1,0:T(8,128)}) %all-gather.13.cloned.1.call-update) | async-done | bytes 1048592 | tf_op jit(solution)/shard_map/all_gather | solution.py:51
  630.3 23.8 %while.47 = (s32[]{:T(128)}, f32[32,32,256]{2,1,0:T(8,128)S(1)}, s32[]{:T(128)}, f32[32,256,256]{2,1,0:T(8,128)}, s32[32]{0:T(128)S(1)}, /*index=5*/f32[32,32,25...) while((s32[]{:T(128)}, f32[32,32,256]{2,1,0:T(8,128)S(1)}, ...), condition=%wide.region_13.15_spmd.clone, body=%wide.region_12.14_spmd.clone.sunk | while | flops 226821696 | bytes 5509559 | solution.py:34
  631.6 3.6 fusion.141
  637.6 3.6 fusion.141
  643.5 3.6 fusion.141
  649.5 3.6 fusion.141
  655.7 75.7 %reduce-scatter.11.cloned.1.call-done = f32[32,512]{1,0:T(8,128)} async-done(((f32[32,8192]{1,0:T(8,128)}), f32[32,512]{1,0:T(8,128)}) %reduce-scatter.11.cloned.1.call-update) | async-done | bytes 65552 | tf_op jit(solution)/shard_map/reduce_scatter | solution.py:54
  732.4 77.3 %psum.7 = f32[32,32]{1,0:T(8,128)S(1)} all-reduce(f32[32,32]{1,0:T(8,128)S(1)} %fusion.80), channel_id=1, replica_groups=mesh['row'=16,'col'=16] {'row','col'}, use_global_device_ids=true, to_apply=%region_15.17 | all-reduce | flops 1024 | bytes 8192 | tf_op jit(solution)/shard_map/psum | solution.py:71
  (140 shorter events, 76.6 us)
Async XLA Ops:
  7.2 45.4 %all-gather.7.cloned.1.call-start = ((), (), s32[]{:S(2)}) async-start(), calls=%async_computation.4 | async-start | bytes 1114112 | tf_op jit(solution)/shard_map/all_gather | solution.py:51
  7.9 152.5 %reduce-scatter.5.cloned.1.call-start = ((), (), s32[]{:S(2)}) async-start(), calls=%async_computation.5 | async-start | bytes 1114112 | tf_op jit(solution)/shard_map/reduce_scatter | solution.py:54
  54.1 106.3 %copy-start = (f32[32,512]{1,0:T(8,128)S(1)}, f32[32,512]{1,0:T(8,128)}, u32[]{:S(2)}) copy-start(f32[32,512]{1,0:T(8,128)} %param.16) | copy-start | bytes 196612
  54.1 106.3 %copy-start.5 = (f32[512]{0:T(512)S(1)}, f32[512]{0:T(512)}, u32[]{:S(2)}) copy-start(f32[512]{0:T(512)} %param.17) | copy-start | bytes 6148
  84.8 118.2 %all-gather.9.cloned.1.call-start = ((), (), s32[]{:S(2)}) async-start(), calls=%async_computation.6 | async-start | bytes 1114112 | tf_op jit(solution)/shard_map/all_gather | solution.py:51
  161.9 148.8 %reduce-scatter.7.cloned.1.call-start = ((), (), s32[]{:S(2)}) async-start(), calls=%async_computation.7 | async-start | bytes 1114112 | tf_op jit(solution)/shard_map/reduce_scatter | solution.py:54
  204.4 106.3 %copy-start.2 = (f32[32,512]{1,0:T(8,128)S(1)}, f32[32,512]{1,0:T(8,128)}, u32[]{:S(2)}) copy-start(f32[32,512]{1,0:T(8,128)} %reduce-scatter.5.cloned.1.call-done) | copy-start | bytes 196612
  235.0 118.0 %all-gather.11.cloned.1.call-start = ((), (), s32[]{:S(2)}) async-start(), calls=%async_computation.8 | async-start | bytes 1114112 | tf_op jit(solution)/shard_map/all_gather | solution.py:51
  312.3 148.7 %reduce-scatter.9.cloned.1.call-start = ((), (), s32[]{:S(2)}) async-start(), calls=%async_computation.9 | async-start | bytes 1114112 | tf_op jit(solution)/shard_map/reduce_scatter | solution.py:54
  354.5 106.4 %copy-start.3 = (f32[32,512]{1,0:T(8,128)S(1)}, f32[32,512]{1,0:T(8,128)}, u32[]{:S(2)}) copy-start(f32[32,512]{1,0:T(8,128)} %multiply_subtract_fusion.1) | copy-start | bytes 196612
  383.6 246.7 %copy-start.4 = (s32[32]{0:T(128)S(1)}, s32[32]{0:T(128)}, u32[]{:S(2)}) copy-start(s32[32]{0:T(128)} %get-tuple-element.843) | copy-start | bytes 388
  383.6 246.7 %copy-start.6 = (s32[32]{0:T(128)S(1)}, s32[32]{0:T(128)}, u32[]{:S(2)}) copy-start(s32[32]{0:T(128)} %get-tuple-element.851) | copy-start | bytes 388
  385.2 197.3 %all-gather.15.cloned.1.call-start = ((), (), s32[]{:S(2)}) async-start(), calls=%async_computation.12 | async-start | bytes 4210688 | tf_op jit(solution)/shard_map/all_gather | solution.py:13
  462.6 166.2 %all-gather.13.cloned.1.call-start = ((), (), s32[]{:S(2)}) async-start(), calls=%async_computation.10 | async-start | bytes 1114112 | tf_op jit(solution)/shard_map/all_gather | solution.py:51
  592.7 138.7 %reduce-scatter.11.cloned.1.call-start = ((), (), s32[]{:S(2)}) async-start(), calls=%async_computation.11 | async-start | bytes 1114112 | tf_op jit(solution)/shard_map/reduce_scatter | solution.py:54
  630.3 101.1 %copy-start.1 = (f32[32,512]{1,0:T(8,128)S(1)}, f32[32,512]{1,0:T(8,128)}, u32[]{:S(2)}) copy-start(f32[32,512]{1,0:T(8,128)} %fusion.87) | copy-start | bytes 196612
Sparse Core Ops, SparseCore 0:
  9.8 42.7 all-gather.6
  84.9 75.4 reduce-scatter.4
  162.8 40.0 all-gather.8
  235.2 75.5 reduce-scatter.6
  313.0 40.0 all-gather.10
  385.3 75.5 reduce-scatter.8
  465.2 117.2 all-gather.14
  592.8 35.9 all-gather.12
  655.8 75.5 reduce-scatter.10
